TPU v7x, 32 devices: a whole 2x2x4 slice. The times are simulated.
32 devices in a mesh: batch: 4 (over y, x), filt: 8 (over z, core).
Axes of the slice: x: 2, y: 2, z: 4, core: 2. Of those that a mesh axis runs over, the one named last changes fastest.
Arguments:
- images: bfloat16 [768, 3072], P(('batch', 'filt')), may hold values from -6 to 6
- labels: int32 [768], P(('batch', 'filt')), may hold values from 0 to 9
- partner: int32 [768], P(('batch', 'filt')), may hold values from 0 to 767, as said below
- valid_mask: int32 [768], P(('batch', 'filt')), may hold values from 0 to 1, as said below
- group_sizes: int32 [4, 8], replicated, may hold values from 1 to 185, as said below
- stem_weight: float32 [16, 27], replicated, may hold values from -1.25 to 1.25
- bridge_weight: float32 [640, 16], P('filt'), may hold values from -1.5 to 1.5
- conv_weight: float32 [2, 640, 9, 640], P(None, 'filt'), may hold values from -0.078125 to 0.078125
- norm_params: float32 [6, 640], P(None, 'filt'), may hold values from 0.5 to 1.5
- head_weight: float32 [10, 640], P(None, 'filt'), may hold values from -1 to 1
- head_bias: float32 [10], replicated, may hold values from -3 to 3
- stem_first: float32 [16, 27], replicated, may hold values from -4.7683716e-06 to 4.7683716e-06
- stem_second: float32 [16, 27], replicated, may hold values from 1.2540817e-12 to 2.002716e-11
- bridge_first: float32 [640, 16], P('filt'), may hold values from -9.536743e-07 to 9.536743e-07
- bridge_second: float32 [640, 16], P('filt'), may hold values from 5.016327e-14 to 8.010864e-13
- conv_first: float32 [2, 640, 9, 640], P(None, 'filt'), may hold values from -2.3841858e-06 to 2.3841858e-06
- conv_second: float32 [2, 640, 9, 640], P(None, 'filt'), may hold values from 3.5671658e-13 to 5.6966146e-12
- norm_first: float32 [6, 640], P(None, 'filt'), may hold values from -7.6293945e-06 to 7.6293945e-06
- norm_second: float32 [6, 640], P(None, 'filt'), may hold values from 3.2104493e-12 to 5.126953e-11
- head_first: float32 [10, 640], P(None, 'filt'), may hold values from -7.6293945e-06 to 7.6293945e-06
- head_second: float32 [10, 640], P(None, 'filt'), may hold values from 3.2104493e-12 to 5.126953e-11
- bias_first: float32 [10], replicated, may hold values from -2.2888184e-05 to 2.2888184e-05
- bias_second: float32 [10], replicated, may hold values from 3.5671657e-11 to 5.696615e-10
Outputs:
- stem_weight_new: float32 [16, 27], replicated
- stem_first_new: float32 [16, 27], replicated
- stem_second_new: float32 [16, 27], replicated
- bridge_weight_new: float32 [640, 16], P('filt')
- bridge_first_new: float32 [640, 16], P('filt')
- bridge_second_new: float32 [640, 16], P('filt')
- conv_weight_new: float32 [2, 640, 9, 640], P(None, 'filt')
- conv_first_new: float32 [2, 640, 9, 640], P(None, 'filt')
- conv_second_new: float32 [2, 640, 9, 640], P(None, 'filt')
- norm_params_new: float32 [6, 640], P(None, 'filt')
- norm_first_new: float32 [6, 640], P(None, 'filt')
- norm_second_new: float32 [6, 640], P(None, 'filt')
- head_weight_new: float32 [10, 640], P(None, 'filt')
- head_first_new: float32 [10, 640], P(None, 'filt')
- head_second_new: float32 [10, 640], P(None, 'filt')
- head_bias_new: float32 [10], replicated
- bias_first_new: float32 [10], replicated
- bias_second_new: float32 [10], replicated
- grad_norm: float32 [], replicated
- loss: float32 [], replicated
Inputs may be any that keep to these rules, and one draw needn't show every extreme that they name: `group_sizes`: row b lists the sizes of the 8 groups of batch shard b, laid one after another from the shard's first slot; a shard's sizes sum to at most 192, and in one shard exactly. `valid_mask`: slots after a shard's groups hold 0; the first slot of every group holds 1, and so does image 768 - 1. `partner`: each entry is the index of an image whose valid_mask is 1.
All inputs are finite; a program needn't handle non-finite values.
Results may differ from a plain program's by a relative error of at most 0.008.
The roundings to bfloat16 on the way count: a program that leaves them out, or rounds other values in their place, can miss the bound.
Values may be sent and summed in bfloat16 or wider, within the bound.
A program may use at most 256 MiB of HBM per device.

v0:
```python
import jax
import jax.numpy as jnp
from jax import lax
from jax.sharding import PartitionSpec as P

STEP = 8
beta_one = 0.9
beta_two = 0.95
adam_eps = 1e-08
norm_epsilon = 1e-05
clip_norm = 0.01
own_share = 0.7


def make_patches(images):
    number = images.shape[0]
    grid = images.reshape(number, 3, 32, 32)
    padded = jnp.pad(grid, ((0, 0), (0, 0), (1, 1), (1, 1)))
    pieces = [
        padded[:, :, row_off : row_off + 29 : 4, col_off : col_off + 29 : 4]
        for row_off in range(3)
        for col_off in range(3)
    ]
    stacked = jnp.stack(pieces, axis=2)
    return jnp.transpose(stacked, (1, 2, 0, 3, 4)).reshape(27, number * 64)


def shifted(feature_field):
    width, rows = feature_field.shape
    grid = feature_field.reshape(width, rows // 64, 8, 8)
    padded = jnp.pad(grid, ((0, 0), (0, 0), (1, 1), (1, 1)))
    pieces = [
        padded[:, :, row_off : row_off + 8, col_off : col_off + 8]
        for row_off in range(3)
        for col_off in range(3)
    ]
    return jnp.stack(pieces, axis=0).reshape(9 * width, rows)


def unshifted(parts, width):
    rows = parts.shape[1]
    grid = parts.reshape(9, width, rows // 64, 8, 8)
    summed = jnp.zeros((width, rows // 64, 10, 10), jnp.float32)
    for row_off in range(3):
        for col_off in range(3):
            summed = summed + jnp.pad(
                grid[3 * row_off + col_off],
                ((0, 0), (0, 0), (row_off, 2 - row_off), (col_off, 2 - col_off)),
            )
    return summed[:, :, 1:9, 1:9].reshape(width, rows)


def image_weights(valid_mask, group_sizes):
    shards, groups = group_sizes.shape
    capacity = valid_mask.shape[0] // shards
    group_ends = jnp.cumsum(group_sizes, axis=1)
    slot_index = jnp.arange(capacity, dtype=jnp.int32)
    member = jnp.sum(
        (slot_index[None, :, None] >= group_ends[:, None, :]).astype(jnp.int32), axis=2
    )
    member = jnp.minimum(member, groups - 1)
    chosen = (member[:, :, None] == jnp.arange(groups, dtype=jnp.int32)[None, None, :]).astype(
        jnp.float32
    )
    sizes_each = jnp.sum(chosen * group_sizes[:, None, :].astype(jnp.float32), axis=2)
    return valid_mask.astype(jnp.float32) / sizes_each.reshape(-1)


def norm_forward(feature_field, norm_gain, norm_shift, row_validity_mask, valid_count):
    batch_mean = (
        lax.psum(jnp.sum(feature_field * row_validity_mask, axis=1), ("batch", "filt"))
        / valid_count
    )
    centered_input = feature_field - batch_mean[:, None]
    batch_variance = (
        lax.psum(
            jnp.sum(centered_input * centered_input * row_validity_mask, axis=1), ("batch", "filt")
        )
        / valid_count
    )
    inverse_scale = lax.rsqrt(batch_variance + norm_epsilon)
    normalized_input = (feature_field - batch_mean[:, None]) * inverse_scale[:, None]
    norm_output = jnp.maximum(norm_gain[:, None] * normalized_input + norm_shift[:, None], 0.0)
    return (norm_output, normalized_input, inverse_scale)


def masked_norm_backward(
    output_gradient,
    norm_output,
    normalized_input,
    inverse_scale,
    norm_gain,
    row_validity_mask,
    valid_count,
):
    passed_rows = jnp.where(norm_output > 0.0, output_gradient, 0.0)
    shift_gradient, gain_gradient = lax.psum(
        (jnp.sum(passed_rows, axis=1), jnp.sum(passed_rows * normalized_input, axis=1)),
        ("batch", "filt"),
    )
    input_gradient = (
        passed_rows
        - row_validity_mask[None, :]
        * (shift_gradient[:, None] + normalized_input * gain_gradient[:, None])
        / valid_count
    )
    return ((norm_gain * inverse_scale)[:, None] * input_gradient, gain_gradient, shift_gradient)


def conv_forward(feature_field, weight_shard):
    stacked = shifted(feature_field)
    low_shard = weight_shard.astype(jnp.bfloat16)
    piece = lax.all_gather(low_shard, "filt", axis=0, tiled=True)
    norm_output = jnp.dot(
        piece.reshape(piece.shape[0], -1), stacked, preferred_element_type=jnp.float32
    )
    return (norm_output, None)


def conv_backward(feature_field, weight_shard, output_gradient):
    width = feature_field.shape[0]
    stacked = shifted(feature_field)
    rows_grad = output_gradient
    term = lax.dot_general(
        rows_grad, stacked, (((1,), (1,)), ((), ())), preferred_element_type=jnp.float32
    )
    weight_grad = lax.psum_scatter(
        term.reshape(lax.axis_size("filt") * weight_shard.shape[0], 9, width),
        "filt",
        scatter_dimension=0,
        tiled=True,
    )
    piece = lax.all_gather(weight_shard.astype(jnp.bfloat16), "filt", axis=0, tiled=True)
    rows_grad = output_gradient
    back = lax.dot_general(
        piece.reshape(piece.shape[0], -1),
        rows_grad,
        (((0,), (0,)), ((), ())),
        preferred_element_type=jnp.float32,
    )
    return (unshifted(back, width), weight_grad)


def adam_step(weight, output_gradient, first, second, rate, shrink, factor):
    clipped = output_gradient * factor
    first = beta_one * first + (1.0 - beta_one) * clipped
    second = beta_two * second + (1.0 - beta_two) * clipped * clipped
    ahead = first / (1.0 - beta_one**STEP)
    behind = second / (1.0 - beta_two**STEP)
    return (
        weight - rate * (ahead / (jnp.sqrt(behind) + adam_eps) + shrink * weight),
        first,
        second,
    )


def body(
    images,
    labels,
    partner,
    valid_mask,
    group_sizes,
    stem_weight,
    bridge_weight,
    conv_weight,
    norm_params,
    head_weight,
    head_bias,
    stem_first,
    stem_second,
    bridge_first,
    bridge_second,
    conv_first,
    conv_second,
    norm_first,
    norm_second,
    head_first,
    head_second,
    bias_first,
    bias_second,
):
    width = bridge_weight.shape[0]
    bridge_all, norm_all, head_all = (
        lax.all_gather(bridge_weight, "filt", axis=0, tiled=True),
        lax.all_gather(norm_params, "filt", axis=1, tiled=True),
        lax.all_gather(head_weight, "filt", axis=1, tiled=True),
    )
    labels_all, valid_all = (
        lax.all_gather(labels, ("batch", "filt"), axis=0, tiled=True),
        lax.all_gather(valid_mask, ("batch", "filt"), axis=0, tiled=True),
    )
    weight_all = image_weights(valid_all, group_sizes)
    total = jnp.sum(weight_all)
    valid_count = 64.0 * jnp.sum(valid_all.astype(jnp.float32))
    local = images.shape[0]
    image_weight = lax.dynamic_slice_in_dim(
        weight_all, lax.axis_index(("batch", "filt")) * local, local
    )
    row_validity_mask = jnp.repeat(valid_mask.astype(jnp.float32), 64)
    patch = make_patches(images)
    stem = jnp.dot(
        stem_weight.astype(jnp.bfloat16), patch, preferred_element_type=jnp.float32
    ).astype(jnp.bfloat16)
    base = jnp.dot(bridge_all.astype(jnp.bfloat16), stem, preferred_element_type=jnp.float32)
    first, first_hat, first_scale = norm_forward(
        base, norm_all[0], norm_all[1], row_validity_mask, valid_count
    )
    first_low = first.astype(jnp.bfloat16)
    inner, kept_zero = conv_forward(first_low, conv_weight[0])
    second, second_hat, second_scale = norm_forward(
        inner, norm_all[2], norm_all[3], row_validity_mask, valid_count
    )
    second_low = second.astype(jnp.bfloat16)
    branch, kept_one = conv_forward(second_low, conv_weight[1])
    final, final_hat, final_scale = norm_forward(
        base + branch, norm_all[4], norm_all[5], row_validity_mask, valid_count
    )
    pooled = jnp.mean(final.reshape(final.shape[0], local, 64), axis=2).astype(jnp.bfloat16)
    logits = (
        jnp.dot(head_all.astype(jnp.bfloat16), pooled, preferred_element_type=jnp.float32)
        + head_bias[:, None]
    )
    moved = logits - jnp.max(logits, axis=0, keepdims=True)
    logp = moved - jnp.log(jnp.sum(jnp.exp(moved), axis=0, keepdims=True))
    classes = jnp.arange(logits.shape[0], dtype=jnp.int32)
    partner_labels = jnp.take(labels_all, partner)
    target = own_share * (labels[None, :] == classes[:, None]).astype(jnp.float32) + (
        1.0 - own_share
    ) * (partner_labels[None, :] == classes[:, None]).astype(jnp.float32)
    loss_part = -jnp.sum(image_weight * jnp.sum(target * logp, axis=0))
    d_logits = ((jnp.exp(logp) - target) * (image_weight / total)[None, :]).astype(jnp.bfloat16)
    bias_grad = jnp.sum(d_logits.astype(jnp.float32), axis=1)
    head_grad = lax.dot_general(
        d_logits, pooled, (((1,), (1,)), ((), ())), preferred_element_type=jnp.float32
    )
    d_pooled = lax.dot_general(
        head_all.astype(jnp.bfloat16),
        d_logits,
        (((0,), (0,)), ((), ())),
        preferred_element_type=jnp.float32,
    )
    d_final = jnp.repeat(d_pooled / 64.0, 64, axis=1)
    d_block, gain_two, shift_two = masked_norm_backward(
        d_final, final, final_hat, final_scale, norm_all[4], row_validity_mask, valid_count
    )
    d_second, conv_grad_one = conv_backward(
        second_low, conv_weight[1], d_block.astype(jnp.bfloat16)
    )
    d_inner, gain_one, shift_one = masked_norm_backward(
        d_second, second, second_hat, second_scale, norm_all[2], row_validity_mask, valid_count
    )
    d_first, conv_grad_zero = conv_backward(first_low, conv_weight[0], d_inner.astype(jnp.bfloat16))
    d_lower, gain_zero, shift_zero = masked_norm_backward(
        d_first, first, first_hat, first_scale, norm_all[0], row_validity_mask, valid_count
    )
    d_base = (d_block + d_lower).astype(jnp.bfloat16)
    bridge_grad = lax.dot_general(
        d_base, stem, (((1,), (1,)), ((), ())), preferred_element_type=jnp.float32
    )
    d_stem = lax.dot_general(
        bridge_all.astype(jnp.bfloat16),
        d_base,
        (((0,), (0,)), ((), ())),
        preferred_element_type=jnp.float32,
    ).astype(jnp.bfloat16)
    stem_grad = lax.dot_general(
        d_stem, patch, (((1,), (1,)), ((), ())), preferred_element_type=jnp.float32
    )
    bridge_part, head_part = (
        lax.psum_scatter(bridge_grad, "filt", scatter_dimension=0, tiled=True),
        lax.psum_scatter(head_grad, "filt", scatter_dimension=1, tiled=True),
    )
    conv_grad, bridge_sum, head_sum = lax.psum(
        (jnp.stack([conv_grad_zero, conv_grad_one]), bridge_part, head_part), "batch"
    )
    stem_sum, bias_sum, loss_sum = lax.psum((stem_grad, bias_grad, loss_part), ("batch", "filt"))
    norm_full = jnp.stack([gain_zero, shift_zero, gain_one, shift_one, gain_two, shift_two])
    norm_grad = lax.dynamic_slice_in_dim(norm_full, lax.axis_index("filt") * width, width, 1)
    owned_square = (
        jnp.sum(conv_grad * conv_grad)
        + jnp.sum(bridge_sum * bridge_sum)
        + jnp.sum(norm_grad * norm_grad)
        + jnp.sum(head_sum * head_sum)
    )
    squares_all = (
        lax.psum(owned_square, "filt") + jnp.sum(stem_sum * stem_sum) + jnp.sum(bias_sum * bias_sum)
    )
    grad_norm = jnp.sqrt(squares_all)
    factor = clip_norm / jnp.maximum(grad_norm, clip_norm)
    stem_new = adam_step(stem_weight, stem_sum, stem_first, stem_second, 0.5, 0.05, factor)
    bridge_new = adam_step(
        bridge_weight, bridge_sum, bridge_first, bridge_second, 0.6, 0.05, factor
    )
    conv_new = adam_step(conv_weight, conv_grad, conv_first, conv_second, 0.033, 0.05, factor)
    norm_new = adam_step(norm_params, norm_grad, norm_first, norm_second, 0.5, 0.0, factor)
    head_new = adam_step(head_weight, head_sum, head_first, head_second, 0.1, 0.05, factor)
    bias_new = adam_step(head_bias, bias_sum, bias_first, bias_second, 0.5, 0.0, factor)
    return (
        stem_new[0],
        stem_new[1],
        stem_new[2],
        bridge_new[0],
        bridge_new[1],
        bridge_new[2],
        conv_new[0],
        conv_new[1],
        conv_new[2],
        norm_new[0],
        norm_new[1],
        norm_new[2],
        head_new[0],
        head_new[1],
        head_new[2],
        bias_new[0],
        bias_new[1],
        bias_new[2],
        grad_norm,
        loss_sum / total,
    )


def solution(mesh):
    in_specs = (
        P(("batch", "filt"), None),
        P(("batch", "filt")),
        P(("batch", "filt")),
        P(("batch", "filt")),
        P(),
        P(),
        P("filt", None),
        P(None, "filt", None, None),
        P(None, "filt"),
        P(None, "filt"),
        P(),
        P(),
        P(),
        P("filt", None),
        P("filt", None),
        P(None, "filt", None, None),
        P(None, "filt", None, None),
        P(None, "filt"),
        P(None, "filt"),
        P(None, "filt"),
        P(None, "filt"),
        P(),
        P(),
    )
    out_specs = (
        P(),
        P(),
        P(),
        P("filt", None),
        P("filt", None),
        P("filt", None),
        P(None, "filt", None, None),
        P(None, "filt", None, None),
        P(None, "filt", None, None),
        P(None, "filt"),
        P(None, "filt"),
        P(None, "filt"),
        P(None, "filt"),
        P(None, "filt"),
        P(None, "filt"),
        P(),
        P(),
        P(),
        P(),
        P(),
    )
    return jax.shard_map(body, mesh=mesh, in_specs=in_specs, out_specs=out_specs, check_vma=False)
```

profile of v0, /device:TPU:0, one launch (start us, length us, event | category | flops | bytes accessed | tf_op | source)
XLA Modules:
  0.0 1185.0 jit_solution(9924384892840319865)
XLA Ops:
  22.0 15.9 %all-gather.3 = bf16[8,80,16]{1,2,0:T(8,128)(2,1)S(1)} all-gather(bf16[1,80,16]{1,2,0:T(8,128)(2,1)S(1)} %bitcast_convert_fusion.1), channel_id=1, replica_groups=mesh['batch'=4,'filt'=8] {'filt'}, dimensions={0}, use_global_device_ids=true | all-gather | bytes 23040 | tf_op jit(solution)/shard_map/all_gather | solution.py:184
  53.4 42.8 %all-reduce.23 = (s32[768]{0:T(1024)S(1)}, s32[768]{0:T(1024)S(1)}) all-reduce(s32[768]{0:T(1024)S(1)} %dynamic-update-slice, s32[768]{0:T(1024)S(1)} %dynamic-update-slice.1), channel_id=1, replica_groups=mesh['batch'=4,'filt'=8] {'batch','filt'}, use_global_device_ids=true, to_apply=%add.21 | all-reduce | flops 1536 | bytes 12288
  100.1 43.6 %psum.133 = f32[640]{0:T(1024)S(1)} all-reduce(f32[640]{0:T(1024)S(1)} %get-tuple-element.111), channel_id=1, replica_groups=mesh['batch'=4,'filt'=8] {'batch','filt'}, use_global_device_ids=true, to_apply=%region_1.2 | all-reduce | flops 640 | bytes 5120 | tf_op jit(solution)/shard_map/psum | solution.py:71
  146.4 41.4 %psum.134 = f32[640]{0:T(1024)S(1)} all-reduce(f32[640]{0:T(1024)S(1)} %multiply_reduce_fusion.4), channel_id=1, replica_groups=mesh['batch'=4,'filt'=8] {'batch','filt'}, use_global_device_ids=true, to_apply=%region_4.5 | all-reduce | flops 640 | bytes 5120 | tf_op jit(solution)/shard_map/psum | solution.py:76
  249.3 20.4 %multiply_reduce_fusion.3 = (f32[640]{0:T(1024)S(1)}, f32[1536,640]{1,0:T(8,128)}) fusion(f32[1536]{0:T(1024)S(1)} %mul.497, bf16[5760,1536]{0,1:T(8,128)(2,1)} %bitcast.334, bf16[640,5760]{0,1:T(8,128)(2,1)} %bitcast.371), kind=kOutput, calls=%fused_computation.73 | convolution fusion | flops 11326585856 | bytes 29008384 | tf_op jit(solution)/shard_map/dot_general | solution.py:114
  269.7 38.4 %psum.135 = f32[640]{0:T(1024)S(1)} all-reduce(f32[640]{0:T(1024)S(1)} %get-tuple-element.113), channel_id=1, replica_groups=mesh['batch'=4,'filt'=8] {'batch','filt'}, use_global_device_ids=true, to_apply=%region_6.7 | all-reduce | flops 640 | bytes 5120 | tf_op jit(solution)/shard_map/psum | solution.py:71
  310.8 41.8 %psum.136 = f32[640]{0:T(1024)S(1)} all-reduce(f32[640]{0:T(1024)S(1)} %multiply_reduce_fusion.2), channel_id=1, replica_groups=mesh['batch'=4,'filt'=8] {'batch','filt'}, use_global_device_ids=true, to_apply=%region_8.9 | all-reduce | flops 640 | bytes 5120 | tf_op jit(solution)/shard_map/psum | solution.py:76
  379.4 20.7 %multiply_reduce_fusion.1 = (f32[640]{0:T(1024)S(1)}, f32[1536,640]{1,0:T(8,128)}) fusion(f32[1536]{0:T(1024)S(1)} %mul.497, f32[1536,640]{1,0:T(8,128)} %get-tuple-element.112, bf16[5760,1536]{0,1:T(8,128)(2,1)} %bitcast.335, bf16[640,5760]{0,1:T(8,128)(2,1)} %bitcast.373), kind=kOutput, calls=%fused_computation.70 | convolution fusion | flops 11327568896 | bytes 32940544 | tf_op jit(solution)/shard_map/dot_general | solution.py:114
  400.1 38.6 %psum.137 = f32[640]{0:T(1024)S(1)} all-reduce(f32[640]{0:T(1024)S(1)} %get-tuple-element.115), channel_id=1, replica_groups=mesh['batch'=4,'filt'=8] {'batch','filt'}, use_global_device_ids=true, to_apply=%region_10.11 | all-reduce | flops 640 | bytes 5120 | tf_op jit(solution)/shard_map/psum | solution.py:71
  441.4 41.9 %psum.138 = f32[640]{0:T(1024)S(1)} all-reduce(f32[640]{0:T(1024)S(1)} %multiply_reduce_fusion), channel_id=1, replica_groups=mesh['batch'=4,'filt'=8] {'batch','filt'}, use_global_device_ids=true, to_apply=%region_12.13 | all-reduce | flops 640 | bytes 5120 | tf_op jit(solution)/shard_map/psum | solution.py:76
  495.4 38.8 %all-reduce.27 = (f32[640]{0:T(1024)S(1)}, f32[640]{0:T(1024)S(1)}) all-reduce(f32[640]{0:T(1024)S(1)} %get-tuple-element.25, f32[640]{0:T(1024)S(1)} %get-tuple-element.24), channel_id=1, replica_groups=mesh['batch'=4,'filt'=8] {'batch','filt'}, use_global_device_ids=true, to_apply=%region_23.24 | all-reduce | flops 1280 | bytes 10240 | tf_op jit(solution)/shard_map/psum | solution.py:97
  539.9 24.1 %convolution_bitcast_fusion.1 = f32[5760,1536]{0,1:T(8,128)} fusion(bf16[640,5760]{0,1:T(8,128)(2,1)} %bitcast.374, f32[640,1536]{0,1:T(8,128)} %fusion.4), kind=kOutput, calls=%fused_computation.2 | convolution fusion | flops 11325603840 | bytes 46694400 | tf_op jit(solution)/shard_map/dot_general | solution.py:135
  564.0 22.5 %fusion.63 = (f32[640,1536]{0,1:T(8,128)}, f32[640,1536]{0,1:T(8,128)S(1)}, f32[640,1536]{0,1:T(8,128)}, f32[640,1536]{0,1:T(8,128)}, f32[640,1536]{0,1:T(8,128)...) fusion(f32[5760,1536]{0,1:T(8,128)} %convolution_bitcast_fusion.1), kind=kLoop, calls=%fused_computation.220 | loop fusion | bytes 70778880 | tf_op jit(solution)/shard_map/slice | solution.py:47
  609.1 41.4 %all-reduce.26 = (f32[640]{0:T(1024)S(1)}, f32[640]{0:T(1024)S(1)}) all-reduce(f32[640]{0:T(1024)S(1)} %get-tuple-element.23, f32[640]{0:T(1024)S(1)} %get-tuple-element.22), channel_id=1, replica_groups=mesh['batch'=4,'filt'=8] {'batch','filt'}, use_global_device_ids=true, to_apply=%region_27.28 | all-reduce | flops 1280 | bytes 10240 | tf_op jit(solution)/shard_map/psum | solution.py:97
  656.0 18.0 %fusion.31 = f32[640,9,640]{2,0,1:T(8,128)} fusion(bf16[9,640,1536]{1,2,0:T(8,128)(2,1)} %constant_dynamic-update-slice_fusion.11, bf16[640,1536]{0,1:T(8,128)(2,1)S(1)} %fusion.24), kind=kOutput, calls=%fused_computation.96 | convolution fusion | flops 11324620800 | bytes 34406400 | tf_op jit(solution)/shard_map/dot_general | solution.py:124
  692.6 18.0 %fusion.29 = f32[640,9,640]{2,0,1:T(8,128)} fusion(bf16[9,640,1536]{1,2,0:T(8,128)(2,1)} %constant_dynamic-update-slice_fusion.19, f32[640,1536]{0,1:T(8,128)S(1)} %copy-done.6), kind=kOutput, calls=%fused_computation.93 | convolution fusion | flops 11325603840 | bytes 36372480 | tf_op jit(solution)/shard_map/dot_general | solution.py:124
  712.1 21.5 %convolution_bitcast_fusion = f32[5760,1536]{0,1:T(8,128)} fusion(bf16[640,1536]{0,1:T(8,128)(2,1)S(1)} %copy-done.8, bf16[640,5760]{0,1:T(8,128)(2,1)} %bitcast.372), kind=kOutput, calls=%fused_computation.1 | convolution fusion | flops 11324620800 | bytes 44728320 | tf_op jit(solution)/shard_map/dot_general | solution.py:135
  733.6 24.1 %fusion.62 = (f32[640,1536]{0,1:T(8,128)}, f32[640,1536]{0,1:T(8,128)}, f32[640,1536]{0,1:T(8,128)}, f32[640,1536]{0,1:T(8,128)}, f32[640,1536]{0,1:T(8,128)}, /...) fusion(f32[5760,1536]{0,1:T(8,128)} %convolution_bitcast_fusion), kind=kLoop, calls=%fused_computation.219 | loop fusion | bytes 70778880 | tf_op jit(solution)/shard_map/slice | solution.py:47
  775.5 40.8 %all-reduce.25 = (f32[640]{0:T(1024)S(1)}, f32[640]{0:T(1024)S(1)}) all-reduce(f32[640]{0:T(1024)S(1)} %get-tuple-element.21, f32[640]{0:T(1024)S(1)} %get-tuple-element.20), channel_id=1, replica_groups=mesh['batch'=4,'filt'=8] {'batch','filt'}, use_global_device_ids=true, to_apply=%region_31.32 | all-reduce | flops 1280 | bytes 10240 | tf_op jit(solution)/shard_map/psum | solution.py:97
  825.0 149.3 %reduce-scatter.11.cloned.1.call-done = f32[80,9,640]{2,0,1:T(8,128)} async-done(((f32[640,9,640]{2,0,1:T(8,128)}), f32[80,9,640]{2,0,1:T(8,128)}) %reduce-scatter.11.cloned.1.call-update) | async-done | bytes 1843216 | tf_op jit(solution)/shard_map/reduce_scatter | solution.py:127
  982.4 38.0 %all-reduce.24 = (f32[16,27]{1,0:T(8,128)S(1)}, f32[10]{0:T(128)S(1)}, f32[]{:T(128)}) all-reduce(f32[16,27]{1,0:T(8,128)S(1)} %fusion.36, f32[10]{0:T(128)S(1)} %copy-done.53, f32[]{:T(128)S(6)} %neg.3), channel_id=1, replica_groups=mesh['batch'=4,'filt'=8] {'batch','filt'}, use_global_device_ids=true, to_apply=%region_32.33 | all-reduce | flops 443 | bytes 3544 | tf_op jit(solution)/shard_map/psum | solution.py:276
  1038.4 16.5 %all-reduce.28 = (f32[80,16]{0,1:T(8,128)S(1)}, f32[10,80]{1,0:T(8,128)S(1)}) all-reduce(f32[80,16]{0,1:T(8,128)S(1)} %copy.169, f32[10,80]{1,0:T(8,128)S(1)} %copy.171), channel_id=1, replica_groups=mesh['batch'=4,'filt'=8] {'batch'}, use_global_device_ids=true, to_apply=%region_38.39 | all-reduce | flops 2080 | bytes 16640 | tf_op jit(solution)/shard_map/psum | solution.py:273
  1056.1 79.8 %all-reduce.31.cloned.1.call-done = f32[2,80,9,640]{3,1,2,0:T(8,128)} async-done(((f32[2,80,9,640]{3,1,2,0:T(8,128)}), f32[2,80,9,640]{3,1,2,0:T(8,128)}) %all-reduce.31.cloned.1.call-update) | async-done | bytes 3686416 | tf_op jit(solution)/shard_map/psum | solution.py:273
  1143.4 16.9 %psum.149 = f32[]{:T(128)} all-reduce(f32[]{:T(128)S(6)} %add.378), channel_id=1, replica_groups=mesh['batch'=4,'filt'=8] {'filt'}, use_global_device_ids=true, to_apply=%region_44.45 | all-reduce | flops 1 | bytes 8 | tf_op jit(solution)/shard_map/psum | solution.py:286
  (291 shorter events, 264.5 us)
Async XLA Ops:
  7.2 229.8 %all-gather.8.cloned.1.call-start = ((), (), s32[]{:S(2)}) async-start(), calls=%async_computation.7 | async-start | bytes 8294400 | tf_op jit(solution)/shard_map/all_gather | solution.py:113
  10.9 356.1 %all-gather.10.cloned.1.call-start = ((), (), s32[]{:S(2)}) async-start(), calls=%async_computation.8 | async-start | bytes 8294400 | tf_op jit(solution)/shard_map/all_gather | solution.py:113
  11.7 813.3 %reduce-scatter.9.cloned.1.call-start = ((), (), s32[]{:S(2)}) async-start(), calls=%async_computation.4 | async-start | bytes 16588800 | tf_op jit(solution)/shard_map/reduce_scatter | solution.py:127
  21.8 124.6 %copy-start.9 = (bf16[27,1536]{1,0:T(8,128)(2,1)}, bf16[27,1536]{1,0:T(8,128)(2,1)S(1)}, u32[]{:S(2)}) copy-start(bf16[27,1536]{1,0:T(8,128)(2,1)S(1)} %reshape.217) | copy-start | bytes 248836
  96.8 121.9 %copy-start.48 = (f32[768]{0:T(1024)}, f32[768]{0:T(1024)S(1)}, u32[]{:S(2)}) copy-start(f32[768]{0:T(1024)S(1)} %get-tuple-element.72) | copy-start | bytes 9220
  674.1 300.3 %reduce-scatter.11.cloned.1.call-start = ((), (), s32[]{:S(2)}) async-start(), calls=%async_computation.5 | async-start | bytes 16588800 | tf_op jit(solution)/shard_map/reduce_scatter | solution.py:127
  710.6 311.0 %reduce-scatter.15.cloned.1.call-start = ((), (), s32[]{:S(2)}) async-start(), calls=%async_computation.10 | async-start | bytes 368640
  817.3 220.2 %reduce-scatter.13.cloned.1.call-start = ((), (), s32[]{:S(2)}) async-start(), calls=%async_computation.9 | async-start | bytes 368640
  824.7 311.2 %all-reduce.31.cloned.1.call-start = ((), (), s32[]{:S(2)}) async-start(), calls=%async_computation.6 | async-start | bytes 7372800 | tf_op jit(solution)/shard_map/psum | solution.py:273
  978.6 183.7 %copy-start.52 = (f32[10]{0:T(128)S(1)}, f32[10]{0:T(128)}, u32[]{:S(2)}) copy-start(f32[10]{0:T(128)} %param.33) | copy-start | bytes 124
  978.6 183.7 %copy-start.56 = (f32[10]{0:T(128)S(1)}, f32[10]{0:T(128)}, u32[]{:S(2)}) copy-start(f32[10]{0:T(128)} %param.44) | copy-start | bytes 124
  978.6 183.7 %copy-start.57 = (f32[10]{0:T(128)S(1)}, f32[10]{0:T(128)}, u32[]{:S(2)}) copy-start(f32[10]{0:T(128)} %param.45) | copy-start | bytes 124
  978.7 184.2 %copy-start.31 = (f32[10,80]{1,0:T(8,128)S(1)}, f32[10,80]{1,0:T(8,128)}, u32[]{:S(2)}) copy-start(f32[10,80]{1,0:T(8,128)} %param.32) | copy-start | bytes 9604
  978.7 184.2 %copy-start.41 = (f32[10,80]{1,0:T(8,128)S(1)}, f32[10,80]{1,0:T(8,128)}, u32[]{:S(2)}) copy-start(f32[10,80]{1,0:T(8,128)} %param.42) | copy-start | bytes 9604
  978.7 184.2 %copy-start.42 = (f32[10,80]{1,0:T(8,128)S(1)}, f32[10,80]{1,0:T(8,128)}, u32[]{:S(2)}) copy-start(f32[10,80]{1,0:T(8,128)} %param.43) | copy-start | bytes 9604
  978.7 184.8 %copy-start.40 = (f32[6,80]{1,0:T(8,128)S(1)}, f32[6,80]{1,0:T(8,128)}, u32[]{:S(2)}) copy-start(f32[6,80]{1,0:T(8,128)} %param.31) | copy-start | bytes 5764
  978.7 184.8 %copy-start.49 = (f32[6,80]{1,0:T(8,128)S(1)}, f32[6,80]{1,0:T(8,128)}, u32[]{:S(2)}) copy-start(f32[6,80]{1,0:T(8,128)} %param.40) | copy-start | bytes 5764
  978.7 184.8 %copy-start.50 = (f32[6,80]{1,0:T(8,128)S(1)}, f32[6,80]{1,0:T(8,128)}, u32[]{:S(2)}) copy-start(f32[6,80]{1,0:T(8,128)} %param.41) | copy-start | bytes 5764
  978.7 185.5 %copy-start.33 = (f32[80,16]{0,1:T(8,128)S(1)}, f32[80,16]{0,1:T(8,128)}, u32[]{:S(2)}) copy-start(f32[80,16]{0,1:T(8,128)} %param.29) | copy-start | bytes 15364
  978.7 185.5 %copy-start.43 = (f32[80,16]{0,1:T(8,128)S(1)}, f32[80,16]{0,1:T(8,128)}, u32[]{:S(2)}) copy-start(f32[80,16]{0,1:T(8,128)} %param.36) | copy-start | bytes 15364
  978.8 185.5 %copy-start.44 = (f32[80,16]{0,1:T(8,128)S(1)}, f32[80,16]{0,1:T(8,128)}, u32[]{:S(2)}) copy-start(f32[80,16]{0,1:T(8,128)} %param.37) | copy-start | bytes 15364
  978.8 186.1 %copy-start.29 = (f32[16,27]{1,0:T(8,128)S(1)}, f32[16,27]{1,0:T(8,128)}, u32[]{:S(2)}) copy-start(f32[16,27]{1,0:T(8,128)} %param.28) | copy-start | bytes 5188
  978.8 186.1 %copy-start.45 = (f32[16,27]{1,0:T(8,128)S(1)}, f32[16,27]{1,0:T(8,128)}, u32[]{:S(2)}) copy-start(f32[16,27]{1,0:T(8,128)} %param.34) | copy-start | bytes 5188
  978.8 186.1 %copy-start.46 = (f32[16,27]{1,0:T(8,128)S(1)}, f32[16,27]{1,0:T(8,128)}, u32[]{:S(2)}) copy-start(f32[16,27]{1,0:T(8,128)} %param.35) | copy-start | bytes 5188
  (43 other events, 898.7 us)
Sparse Core Ops, SparseCore 0:
  11.0 77.6 all-gather.7
  90.9 73.2 all-gather.9
  674.2 149.9 reduce-scatter.8
  826.4 147.9 reduce-scatter.10
  977.1 28.8 reduce-scatter.14
  1008.8 28.7 reduce-scatter.12
  1041.2 94.6 all-reduce.30
where the time goes:
time: 1190 us; the launch traced here: 1180 us
  blocking collectives  526 us (44%)
  waiting for transfers between devices  245 us (21%)
  local copies, waits for them, and re-layouts  146 us (12%)
  matrix products  129 us (11%)
  other arithmetic  113 us (9%)
  between operations  25.3 us (2%)
    reduce_scatter x2, waiting for transfers between devices, conv_backward(): lax.psum_scatter(term.reshape(lax.axis_size('filt') * weight_shard.shape[...  149 us
    psum x3, blocking collectives, norm_forward(): lax.psum(jnp.sum(centered_input * centered_input * row_validity_mask, axi...  125 us
    psum x3, blocking collectives, masked_norm_backward(): lax.psum((jnp.sum(passed_rows, axis=1), jnp.sum(passed_rows * normalized_...  121 us
    psum x3, blocking collectives, norm_forward(): lax.psum(jnp.sum(feature_field * row_validity_mask, axis=1), ('batch', 'f...  121 us
    psum x1, waiting for transfers between devices, body(): lax.psum((jnp.stack([conv_grad_zero, conv_grad_one]), bridge_part, head_p...  79.8 us
    unnamed x168, local copies, waits for them, and re-layouts  52.3 us
    slice x2, local copies, waits for them, and re-layouts, unshifted(): grid[3 * row_off + col_off]  46.7 us
    dot_general x2, matrix products, conv_backward(): lax.dot_general(piece.reshape(piece.shape[0], -1), rows_grad, (((0,), (0,...  45.6 us
  transfers between devices with their start and end apart: 7, of which 3 were waited for; matrix products, arithmetic and copies ran while one was open for 18% of the time, Pallas kernels for 0%

commit v1 on v0

--- a/solution.py
+++ b/solution.py
@@ -68,7 +68,10 @@
 
 def norm_forward(feature_field, norm_gain, norm_shift, row_validity_mask, valid_count):
     batch_mean = (
-        lax.psum(jnp.sum(feature_field * row_validity_mask, axis=1), ("batch", "filt"))
+        jnp.sum(
+            lax.all_gather(jnp.sum(feature_field * row_validity_mask, axis=1), ("batch", "filt")),
+            axis=0,
+        )
         / valid_count
     )
     centered_input = feature_field - batch_mean[:, None]

time: 1190 us -> 1190 us (level)
    all_gather x0 -> x3, blocking collectives: none -> 124 us  [norm_forward(): lax.all_gather(jnp.sum(feature_field * row_validity_mask, axis=1), ('batc...]
    psum x3 -> x0, blocking collectives: 121 us -> none  [norm_forward(): lax.psum(jnp.sum(feature_field * row_validity_mask, axis=1), ('batch', 'f...]
    unnamed x168 -> x171, local copies, waits for them, and re-layouts: 52.3 us -> 52.6 us
where the time goes in v1:
time: 1190 us; the launch traced here: 1180 us
  blocking collectives  521 us (44%)
  waiting for transfers between devices  244 us (21%)
  local copies, waits for them, and re-layouts  147 us (12%)
  matrix products  129 us (11%)
  other arithmetic  114 us (10%)
  between operations  25.3 us (2%)
    reduce_scatter x2, waiting for transfers between devices, conv_backward(): lax.psum_scatter(term.reshape(lax.axis_size('filt') * weight_shard.shape[...  149 us
    all_gather x3, blocking collectives, norm_forward(): lax.all_gather(jnp.sum(feature_field * row_validity_mask, axis=1), ('batc...  124 us
    psum x3, blocking collectives, masked_norm_backward(): lax.psum((jnp.sum(passed_rows, axis=1), jnp.sum(passed_rows * normalized_...  124 us
    psum x3, blocking collectives, norm_forward(): lax.psum(jnp.sum(centered_input * centered_input * row_validity_mask, axi...  114 us
    psum x1, waiting for transfers between devices, body(): lax.psum((jnp.stack([conv_grad_zero, conv_grad_one]), bridge_part, head_p...  80 us
    unnamed x171, local copies, waits for them, and re-layouts  52.6 us
    slice x2, local copies, waits for them, and re-layouts, unshifted(): grid[3 * row_off + col_off]  46.8 us
    dot_general x2, matrix products, conv_backward(): lax.dot_general(piece.reshape(piece.shape[0], -1), rows_grad, (((0,), (0,...  45.5 us
  transfers between devices with their start and end apart: 7, of which 3 were waited for; matrix products, arithmetic and copies ran while one was open for 18% of the time, Pallas kernels for 0%

profile of v1, /device:TPU:0, one launch (start us, length us, event | category | flops | bytes accessed | tf_op | source)
XLA Modules:
  0.0 1179.7 jit_solution(1593218497821096237)
XLA Ops:
  22.0 15.8 %all-gather.6 = bf16[8,80,16]{1,2,0:T(8,128)(2,1)S(1)} all-gather(bf16[1,80,16]{1,2,0:T(8,128)(2,1)S(1)} %bitcast_convert_fusion.1), channel_id=1, replica_groups=mesh['batch'=4,'filt'=8] {'filt'}, dimensions={0}, use_global_device_ids=true | all-gather | bytes 23040 | tf_op jit(solution)/shard_map/all_gather | solution.py:187
  40.7 43.1 %all-gather.7 = f32[32,1,640]{2,1,0:T(1,128)S(1)} all-gather(f32[1,1,640]{2,1,0:T(1,128)S(1)} %reshape.259), channel_id=2, replica_groups=mesh['batch'=4,'filt'=8] {'batch','filt'}, dimensions={0}, use_global_device_ids=true | all-gather | bytes 84480 | tf_op jit(solution)/shard_map/all_gather | solution.py:72
  98.9 42.7 %all-reduce.23 = (s32[768]{0:T(1024)S(1)}, s32[768]{0:T(1024)S(1)}) all-reduce(s32[768]{0:T(1024)S(1)} %dynamic-update-slice, s32[768]{0:T(1024)S(1)} %dynamic-update-slice.1), channel_id=1, replica_groups=mesh['batch'=4,'filt'=8] {'batch','filt'}, use_global_device_ids=true, to_apply=%add.21 | all-reduce | flops 1536 | bytes 12288
  145.6 40.2 %psum.112 = f32[640]{0:T(1024)S(1)} all-reduce(f32[640]{0:T(1024)S(1)} %multiply_reduce_fusion.4), channel_id=1, replica_groups=mesh['batch'=4,'filt'=8] {'batch','filt'}, use_global_device_ids=true, to_apply=%region_4.5 | all-reduce | flops 640 | bytes 5120 | tf_op jit(solution)/shard_map/psum | solution.py:79
  247.0 20.4 %multiply_reduce_fusion.3 = (f32[640]{0:T(1024)S(1)}, f32[1536,640]{1,0:T(8,128)}) fusion(f32[1536]{0:T(1024)S(1)} %mul.497, bf16[5760,1536]{0,1:T(8,128)(2,1)} %bitcast.334, bf16[640,5760]{0,1:T(8,128)(2,1)} %bitcast.371), kind=kOutput, calls=%fused_computation.73 | convolution fusion | flops 11326585856 | bytes 29008384 | tf_op jit(solution)/shard_map/dot_general | solution.py:117
  267.4 40.6 %all-gather.8 = f32[32,1,640]{2,1,0:T(1,128)S(1)} all-gather(f32[1,1,640]{2,1,0:T(1,128)S(1)} %reshape.261), channel_id=4, replica_groups=mesh['batch'=4,'filt'=8] {'batch','filt'}, dimensions={0}, use_global_device_ids=true | all-gather | bytes 84480 | tf_op jit(solution)/shard_map/all_gather | solution.py:72
  310.7 37.1 %psum.113 = f32[640]{0:T(1024)S(1)} all-reduce(f32[640]{0:T(1024)S(1)} %multiply_reduce_fusion.2), channel_id=1, replica_groups=mesh['batch'=4,'filt'=8] {'batch','filt'}, use_global_device_ids=true, to_apply=%region_8.9 | all-reduce | flops 640 | bytes 5120 | tf_op jit(solution)/shard_map/psum | solution.py:79
  374.7 20.7 %multiply_reduce_fusion.1 = (f32[640]{0:T(1024)S(1)}, f32[1536,640]{1,0:T(8,128)}) fusion(f32[1536]{0:T(1024)S(1)} %mul.497, f32[1536,640]{1,0:T(8,128)} %get-tuple-element.112, bf16[5760,1536]{0,1:T(8,128)(2,1)} %bitcast.335, bf16[640,5760]{0,1:T(8,128)(2,1)} %bitcast.373), kind=kOutput, calls=%fused_computation.70 | convolution fusion | flops 11327568896 | bytes 32940544 | tf_op jit(solution)/shard_map/dot_general | solution.py:117
  395.4 40.6 %all-gather.9 = f32[32,1,640]{2,1,0:T(1,128)S(1)} all-gather(f32[1,1,640]{2,1,0:T(1,128)S(1)} %reshape.263), channel_id=6, replica_groups=mesh['batch'=4,'filt'=8] {'batch','filt'}, dimensions={0}, use_global_device_ids=true | all-gather | bytes 84480 | tf_op jit(solution)/shard_map/all_gather | solution.py:72
  438.7 36.9 %psum.114 = f32[640]{0:T(1024)S(1)} all-reduce(f32[640]{0:T(1024)S(1)} %multiply_reduce_fusion), channel_id=1, replica_groups=mesh['batch'=4,'filt'=8] {'batch','filt'}, use_global_device_ids=true, to_apply=%region_12.13 | all-reduce | flops 640 | bytes 5120 | tf_op jit(solution)/shard_map/psum | solution.py:79
  487.8 42.8 %all-reduce.27 = (f32[640]{0:T(1024)S(1)}, f32[640]{0:T(1024)S(1)}) all-reduce(f32[640]{0:T(1024)S(1)} %get-tuple-element.25, f32[640]{0:T(1024)S(1)} %get-tuple-element.24), channel_id=1, replica_groups=mesh['batch'=4,'filt'=8] {'batch','filt'}, use_global_device_ids=true, to_apply=%region_23.24 | all-reduce | flops 1280 | bytes 10240 | tf_op jit(solution)/shard_map/psum | solution.py:100
  536.3 24.1 %convolution_bitcast_fusion.1 = f32[5760,1536]{0,1:T(8,128)} fusion(bf16[640,5760]{0,1:T(8,128)(2,1)} %bitcast.374, f32[640,1536]{0,1:T(8,128)} %fusion.4), kind=kOutput, calls=%fused_computation.2 | convolution fusion | flops 11325603840 | bytes 46694400 | tf_op jit(solution)/shard_map/dot_general | solution.py:138
  560.4 22.5 %fusion.63 = (f32[640,1536]{0,1:T(8,128)}, f32[640,1536]{0,1:T(8,128)S(1)}, f32[640,1536]{0,1:T(8,128)}, f32[640,1536]{0,1:T(8,128)}, f32[640,1536]{0,1:T(8,128)...) fusion(f32[5760,1536]{0,1:T(8,128)} %convolution_bitcast_fusion.1), kind=kLoop, calls=%fused_computation.220 | loop fusion | bytes 70778880 | tf_op jit(solution)/shard_map/slice | solution.py:47
  605.4 38.6 %all-reduce.26 = (f32[640]{0:T(1024)S(1)}, f32[640]{0:T(1024)S(1)}) all-reduce(f32[640]{0:T(1024)S(1)} %get-tuple-element.23, f32[640]{0:T(1024)S(1)} %get-tuple-element.22), channel_id=1, replica_groups=mesh['batch'=4,'filt'=8] {'batch','filt'}, use_global_device_ids=true, to_apply=%region_27.28 | all-reduce | flops 1280 | bytes 10240 | tf_op jit(solution)/shard_map/psum | solution.py:100
  649.6 18.0 %fusion.31 = f32[640,9,640]{2,0,1:T(8,128)} fusion(bf16[9,640,1536]{1,2,0:T(8,128)(2,1)} %constant_dynamic-update-slice_fusion.11, bf16[640,1536]{0,1:T(8,128)(2,1)S(1)} %fusion.24), kind=kOutput, calls=%fused_computation.96 | convolution fusion | flops 11324620800 | bytes 34406400 | tf_op jit(solution)/shard_map/dot_general | solution.py:127
  686.3 17.9 %fusion.29 = f32[640,9,640]{2,0,1:T(8,128)} fusion(bf16[9,640,1536]{1,2,0:T(8,128)(2,1)} %constant_dynamic-update-slice_fusion.19, f32[640,1536]{0,1:T(8,128)S(1)} %copy-done.6), kind=kOutput, calls=%fused_computation.93 | convolution fusion | flops 11325603840 | bytes 36372480 | tf_op jit(solution)/shard_map/dot_general | solution.py:127
  705.9 21.4 %convolution_bitcast_fusion = f32[5760,1536]{0,1:T(8,128)} fusion(bf16[640,1536]{0,1:T(8,128)(2,1)S(1)} %copy-done.8, bf16[640,5760]{0,1:T(8,128)(2,1)} %bitcast.372), kind=kOutput, calls=%fused_computation.1 | convolution fusion | flops 11324620800 | bytes 44728320 | tf_op jit(solution)/shard_map/dot_general | solution.py:138
  727.2 24.2 %fusion.62 = (f32[640,1536]{0,1:T(8,128)}, f32[640,1536]{0,1:T(8,128)}, f32[640,1536]{0,1:T(8,128)}, f32[640,1536]{0,1:T(8,128)}, f32[640,1536]{0,1:T(8,128)}, /...) fusion(f32[5760,1536]{0,1:T(8,128)} %convolution_bitcast_fusion), kind=kLoop, calls=%fused_computation.219 | loop fusion | bytes 70778880 | tf_op jit(solution)/shard_map/slice | solution.py:47
  769.4 42.5 %all-reduce.25 = (f32[640]{0:T(1024)S(1)}, f32[640]{0:T(1024)S(1)}) all-reduce(f32[640]{0:T(1024)S(1)} %get-tuple-element.21, f32[640]{0:T(1024)S(1)} %get-tuple-element.20), channel_id=1, replica_groups=mesh['batch'=4,'filt'=8] {'batch','filt'}, use_global_device_ids=true, to_apply=%region_31.32 | all-reduce | flops 1280 | bytes 10240 | tf_op jit(solution)/shard_map/psum | solution.py:100
  820.6 148.6 %reduce-scatter.11.cloned.1.call-done = f32[80,9,640]{2,0,1:T(8,128)} async-done(((f32[640,9,640]{2,0,1:T(8,128)}), f32[80,9,640]{2,0,1:T(8,128)}) %reduce-scatter.11.cloned.1.call-update) | async-done | bytes 1843216 | tf_op jit(solution)/shard_map/reduce_scatter | solution.py:130
  977.2 38.0 %all-reduce.24 = (f32[16,27]{1,0:T(8,128)S(1)}, f32[10]{0:T(128)S(1)}, f32[]{:T(128)}) all-reduce(f32[16,27]{1,0:T(8,128)S(1)} %fusion.36, f32[10]{0:T(128)S(1)} %copy-done.53, f32[]{:T(128)S(6)} %neg.3), channel_id=1, replica_groups=mesh['batch'=4,'filt'=8] {'batch','filt'}, use_global_device_ids=true, to_apply=%region_32.33 | all-reduce | flops 443 | bytes 3544 | tf_op jit(solution)/shard_map/psum | solution.py:279
  1033.1 16.3 %all-reduce.28 = (f32[80,16]{0,1:T(8,128)S(1)}, f32[10,80]{1,0:T(8,128)S(1)}) all-reduce(f32[80,16]{0,1:T(8,128)S(1)} %copy.169, f32[10,80]{1,0:T(8,128)S(1)} %copy.171), channel_id=1, replica_groups=mesh['batch'=4,'filt'=8] {'batch'}, use_global_device_ids=true, to_apply=%region_38.39 | all-reduce | flops 2080 | bytes 16640 | tf_op jit(solution)/shard_map/psum | solution.py:276
  1050.7 80.0 %all-reduce.31.cloned.1.call-done = f32[2,80,9,640]{3,1,2,0:T(8,128)} async-done(((f32[2,80,9,640]{3,1,2,0:T(8,128)}), f32[2,80,9,640]{3,1,2,0:T(8,128)}) %all-reduce.31.cloned.1.call-update) | async-done | bytes 3686416 | tf_op jit(solution)/shard_map/psum | solution.py:276
  1138.2 16.9 %psum.125 = f32[]{:T(128)} all-reduce(f32[]{:T(128)S(6)} %add.372), channel_id=1, replica_groups=mesh['batch'=4,'filt'=8] {'filt'}, use_global_device_ids=true, to_apply=%region_44.45 | all-reduce | flops 1 | bytes 8 | tf_op jit(solution)/shard_map/psum | solution.py:289
  (297 shorter events, 264.5 us)
Async XLA Ops:
  7.2 227.4 %all-gather.14.cloned.1.call-start = ((), (), s32[]{:S(2)}) async-start(), calls=%async_computation.7 | async-start | bytes 8294400 | tf_op jit(solution)/shard_map/all_gather | solution.py:116
  10.9 351.4 %all-gather.16.cloned.1.call-start = ((), (), s32[]{:S(2)}) async-start(), calls=%async_computation.8 | async-start | bytes 8294400 | tf_op jit(solution)/shard_map/all_gather | solution.py:116
  11.7 808.9 %reduce-scatter.9.cloned.1.call-start = ((), (), s32[]{:S(2)}) async-start(), calls=%async_computation.4 | async-start | bytes 16588800 | tf_op jit(solution)/shard_map/reduce_scatter | solution.py:130
  21.8 123.8 %copy-start.9 = (bf16[27,1536]{1,0:T(8,128)(2,1)}, bf16[27,1536]{1,0:T(8,128)(2,1)S(1)}, u32[]{:S(2)}) copy-start(bf16[27,1536]{1,0:T(8,128)(2,1)S(1)} %reshape.223) | copy-start | bytes 248836
  38.1 107.6 %copy-start.13 = (bf16[1536,16]{0,1:T(8,128)(2,1)}, bf16[1536,16]{0,1:T(8,128)(2,1)S(1)}, u32[]{:S(2)}) copy-start(bf16[1536,16]{0,1:T(8,128)(2,1)S(1)} %convolution_convert_fusion.1) | copy-start | bytes 147460
  667.6 301.6 %reduce-scatter.11.cloned.1.call-start = ((), (), s32[]{:S(2)}) async-start(), calls=%async_computation.5 | async-start | bytes 16588800 | tf_op jit(solution)/shard_map/reduce_scatter | solution.py:130
  704.3 312.1 %reduce-scatter.15.cloned.1.call-start = ((), (), s32[]{:S(2)}) async-start(), calls=%async_computation.10 | async-start | bytes 368640
  812.9 219.4 %reduce-scatter.13.cloned.1.call-start = ((), (), s32[]{:S(2)}) async-start(), calls=%async_computation.9 | async-start | bytes 368640
  820.3 310.4 %all-reduce.31.cloned.1.call-start = ((), (), s32[]{:S(2)}) async-start(), calls=%async_computation.6 | async-start | bytes 7372800 | tf_op jit(solution)/shard_map/psum | solution.py:276
  973.4 183.7 %copy-start.52 = (f32[10]{0:T(128)S(1)}, f32[10]{0:T(128)}, u32[]{:S(2)}) copy-start(f32[10]{0:T(128)} %param.33) | copy-start | bytes 124
  973.4 183.7 %copy-start.56 = (f32[10]{0:T(128)S(1)}, f32[10]{0:T(128)}, u32[]{:S(2)}) copy-start(f32[10]{0:T(128)} %param.44) | copy-start | bytes 124
  973.5 183.6 %copy-start.57 = (f32[10]{0:T(128)S(1)}, f32[10]{0:T(128)}, u32[]{:S(2)}) copy-start(f32[10]{0:T(128)} %param.45) | copy-start | bytes 124
  973.5 184.2 %copy-start.31 = (f32[10,80]{1,0:T(8,128)S(1)}, f32[10,80]{1,0:T(8,128)}, u32[]{:S(2)}) copy-start(f32[10,80]{1,0:T(8,128)} %param.32) | copy-start | bytes 9604
  973.5 184.2 %copy-start.41 = (f32[10,80]{1,0:T(8,128)S(1)}, f32[10,80]{1,0:T(8,128)}, u32[]{:S(2)}) copy-start(f32[10,80]{1,0:T(8,128)} %param.42) | copy-start | bytes 9604
  973.5 184.2 %copy-start.42 = (f32[10,80]{1,0:T(8,128)S(1)}, f32[10,80]{1,0:T(8,128)}, u32[]{:S(2)}) copy-start(f32[10,80]{1,0:T(8,128)} %param.43) | copy-start | bytes 9604
  973.5 184.8 %copy-start.40 = (f32[6,80]{1,0:T(8,128)S(1)}, f32[6,80]{1,0:T(8,128)}, u32[]{:S(2)}) copy-start(f32[6,80]{1,0:T(8,128)} %param.31) | copy-start | bytes 5764
  973.5 184.8 %copy-start.49 = (f32[6,80]{1,0:T(8,128)S(1)}, f32[6,80]{1,0:T(8,128)}, u32[]{:S(2)}) copy-start(f32[6,80]{1,0:T(8,128)} %param.40) | copy-start | bytes 5764
  973.5 184.8 %copy-start.50 = (f32[6,80]{1,0:T(8,128)S(1)}, f32[6,80]{1,0:T(8,128)}, u32[]{:S(2)}) copy-start(f32[6,80]{1,0:T(8,128)} %param.41) | copy-start | bytes 5764
  973.5 185.5 %copy-start.33 = (f32[80,16]{0,1:T(8,128)S(1)}, f32[80,16]{0,1:T(8,128)}, u32[]{:S(2)}) copy-start(f32[80,16]{0,1:T(8,128)} %param.29) | copy-start | bytes 15364
  973.6 185.5 %copy-start.43 = (f32[80,16]{0,1:T(8,128)S(1)}, f32[80,16]{0,1:T(8,128)}, u32[]{:S(2)}) copy-start(f32[80,16]{0,1:T(8,128)} %param.36) | copy-start | bytes 15364
  973.6 185.4 %copy-start.44 = (f32[80,16]{0,1:T(8,128)S(1)}, f32[80,16]{0,1:T(8,128)}, u32[]{:S(2)}) copy-start(f32[80,16]{0,1:T(8,128)} %param.37) | copy-start | bytes 15364
  973.6 186.1 %copy-start.29 = (f32[16,27]{1,0:T(8,128)S(1)}, f32[16,27]{1,0:T(8,128)}, u32[]{:S(2)}) copy-start(f32[16,27]{1,0:T(8,128)} %param.28) | copy-start | bytes 5188
  973.6 186.1 %copy-start.45 = (f32[16,27]{1,0:T(8,128)S(1)}, f32[16,27]{1,0:T(8,128)}, u32[]{:S(2)}) copy-start(f32[16,27]{1,0:T(8,128)} %param.34) | copy-start | bytes 5188
  973.6 186.0 %copy-start.46 = (f32[16,27]{1,0:T(8,128)S(1)}, f32[16,27]{1,0:T(8,128)}, u32[]{:S(2)}) copy-start(f32[16,27]{1,0:T(8,128)} %param.35) | copy-start | bytes 5188
  (43 other events, 883.2 us)
Sparse Core Ops, SparseCore 0:
  11.0 77.2 all-gather.13
  90.5 73.3 all-gather.15
  667.7 151.2 reduce-scatter.8
  821.2 147.9 reduce-scatter.10
  971.9 28.9 reduce-scatter.14
  1003.6 28.6 reduce-scatter.12
  1036.0 94.5 all-reduce.30
